TPU v7x, 512 devices: a whole 4x4x16 slice. The times are simulated.
512 devices in a mesh: snap: 16 (over y, x), plane: 32 (over z, core).
Axes of the slice: x: 4, y: 4, z: 16, core: 2. Of those that a mesh axis runs over, the one named last changes fastest.
Arguments:
- velocity: bfloat16 [16, 128, 3, 128, 128], P('snap', 'plane'), may hold values from -6 to 6
- plane_count: int32 [32], P('plane'), may hold values from 1 to 4, as said below
- inv_span: float32 [32, 4], P('plane'), may hold values from 0.5 to 4
- kernels: float32 [3, 2, 3, 3], replicated, may hold values from -2.4 to 2.4
- omega_block: int32 [32, 4], P('plane'), may hold values from 0 to 7
- omega_table: bfloat16 [8, 9, 32, 256], replicated, may hold values from -0.0625 to 0.0625
- omega_stream: bfloat16 [32, 256], replicated, may hold values from -6 to 6
- wall_shear: bfloat16 [16, 2, 128, 128], P('snap', None, 'plane'), may hold values from -6 to 6
Outputs:
- sketch: float32 [2, 32, 32, 256], P(None, 'plane', 'snap')
- gram: float32 [256, 256], replicated
Inputs may be any that keep to these rules, and one draw needn't show every extreme that they name: `plane_count`: every index of plane holds 1 or more live slots, slots 0 onwards; some index holds 4.
All inputs are finite; a program needn't handle non-finite values.
Results may differ from a plain program's by a relative error of at most 0.0043.
Values may be sent and summed in bfloat16 or wider, within the bound.
No kernel may reach another device: no remote copies, remote signals or barrier semaphores. Data moves between devices by JAX's collectives and lax.ppermute only.
A program may use at most 64 MiB of HBM per device.

v0:
```python
import jax
import jax.numpy as jnp
from jax import lax
from jax.sharding import PartitionSpec as P

X = 128
ZW = 128


def shifted(value, axis, steps):
    count = lax.axis_size(axis)
    leading, last = (max(0, -steps), min(count, count - steps))
    return lax.ppermute(value, axis, [(source, source + steps) for source in range(leading, last)])


def in_plane(centre, kernels):
    snaps, comps, zw, xw = centre.shape
    field = centre.astype(jnp.float32)
    padded = jnp.pad(field, ((0, 0), (0, 0), (1, 1), (1, 1)))
    first = jnp.zeros_like(field)
    second = jnp.zeros_like(field)
    for row_a in range(3):
        for col_b in range(3):
            window = padded[:, :, row_a : row_a + zw, col_b : col_b + xw]
            first = first + kernels[:, 0, row_a, col_b][None, :, None, None] * window
            second = second + kernels[:, 1, row_a, col_b][None, :, None, None] * window
    return (first, second)


def features(centre, below, above, span, kernels):
    snaps, comps, zw, xw = centre.shape
    first, second = in_plane(centre, kernels)
    normal = (above.astype(jnp.float32) - below.astype(jnp.float32)) * span
    grads = jnp.stack([first, second, normal], axis=2).reshape(snaps, 9, zw, xw)
    filtered = grads.reshape(snaps, 9, zw // 4, 4, xw // 4, 4).mean(axis=(3, 5))
    return filtered.astype(jnp.bfloat16)


def per_device(
    velocity, plane_count, inv_span, kernels, omega_block, omega_table, omega_stream, wall_shear
):
    slots = velocity.shape[1]
    live_count = plane_count[0]
    coef = jnp.zeros((velocity.shape[0], omega_stream.shape[1]), jnp.float32)
    last_live = lax.dynamic_index_in_dim(velocity, live_count - 1, 1, keepdims=False)
    from_below = shifted(last_live, "plane", 1)
    from_above = shifted(velocity[:, 0], "plane", -1)
    for slot in range(slots):
        below = from_below if slot == 0 else velocity[:, slot - 1]
        if slot + 1 < slots:
            above = jnp.where(slot + 1 < live_count, velocity[:, slot + 1], from_above)
        else:
            above = from_above
        feats = features(velocity[:, slot], below, above, inv_span[0, slot], kernels)
        proj = jnp.einsum("sczx,xk->sczk", feats, omega_stream, preferred_element_type=jnp.float32)
        table = lax.dynamic_index_in_dim(
            omega_table, omega_block[0, slot], 0, keepdims=False
        ).astype(jnp.float32)
        term = jnp.einsum("sczk,czk->sk", proj, table, precision=lax.Precision.HIGHEST)
        coef = coef + jnp.where(slot < live_count, term, jnp.zeros_like(term))
    coef = lax.psum(coef, "plane")
    snaps, comps, zw, xw = wall_shear.shape
    shear_f = (
        wall_shear.astype(jnp.float32)
        .reshape(snaps, comps, zw // 4, 4, xw // 4, 4)
        .mean(axis=(3, 5))
    )
    partial_sketch = jnp.einsum("smzx,sk->mzxk", shear_f, coef, precision=lax.Precision.HIGHEST)
    sketch = lax.psum_scatter(partial_sketch, "snap", scatter_dimension=2, tiled=True)
    total_rows = 2 * (X // 4) * (ZW // 4)
    flat = sketch.reshape(-1, sketch.shape[-1])
    local_gram = jnp.dot(flat.T, flat, precision=lax.Precision.HIGHEST)
    gram = lax.psum(local_gram, ("snap", "plane")) / jnp.float32(total_rows)
    return (sketch, gram)


def solution(mesh):
    return jax.shard_map(
        per_device,
        mesh=mesh,
        in_specs=(
            P("snap", "plane", None, None, None),
            P("plane"),
            P("plane", None),
            P(),
            P("plane", None),
            P(),
            P(),
            P("snap", None, "plane", None),
        ),
        out_specs=(P(None, "plane", "snap", None), P()),
        check_vma=False,
    )
```

profile of v0, /device:TPU:2, one launch (start us, length us, event | category | flops | bytes accessed | tf_op | source)
XLA Modules:
  0.0 790.4 jit_solution(1391584907513652331)
XLA Ops:
  7.9 1.2 fusion.21
  9.1 1.3 collective-permute-start
  10.4 3.0 collective-permute-start.1
  13.4 0.7 fusion.23
  19.2 0.2 slice_reduce_fusion.17
  19.5 0.1 reduce_sum.53
  19.6 0.1 reduce_sum.54
  22.2 1.3 add_bitcast_fusion.7
  23.6 1.3 add_bitcast_fusion.6
  24.9 0.7 fusion.22
  25.6 2.7 multiply_bitcast_fusion.3
  28.4 21.0 %reshape_reshape.12 = f32[9,32,4,32,4]{4,3,2,1,0:T(8,128)} reshape(f32[1,3,3,128,128]{4,3,2,1,0:T(8,128)S(1)} %copy.14) | data formatting | bytes 1179648 | tf_op jit(solution)/shard_map/reshape;reshape | solution.py:35
  49.5 7.9 %reduce_sum.55 = f32[9,32,32]{2,1,0:T(8,128)S(1)} reduce(f32[9,32,4,32,4]{4,3,2,1,0:T(8,128)} %reshape_reshape.12, f32[]{:T(128)} %constant.38.clone.1), dimensions={2,4}, to_apply=%region_2.3 | reduce | flops 138240 | bytes 626692 | tf_op jit(solution)/shard_map/reduce_sum | solution.py:35
  57.4 20.8 %reshape_reshape.13 = f32[9,32,4,32,4]{4,3,2,1,0:T(8,128)} reshape(f32[1,3,3,128,128]{4,3,2,1,0:T(8,128)S(1)} %copy.15) | data formatting | bytes 1179648 | tf_op jit(solution)/shard_map/reshape;reshape | solution.py:35
  78.3 7.9 %reduce_sum.56 = f32[9,32,32]{2,1,0:T(8,128)S(1)} reduce(f32[9,32,4,32,4]{4,3,2,1,0:T(8,128)} %reshape_reshape.13, f32[]{:T(128)} %constant.38.clone.1), dimensions={2,4}, to_apply=%region_3.4 | reduce | flops 138240 | bytes 626692 | tf_op jit(solution)/shard_map/reduce_sum | solution.py:35
  86.2 0.1 pad_maximum_fusion.2
  86.3 20.8 %reshape_reshape.14 = f32[9,32,4,32,4]{4,3,2,1,0:T(8,128)} reshape(f32[1,3,3,128,128]{4,3,2,1,0:T(8,128)S(1)} %copy.16) | data formatting | bytes 1179648 | tf_op jit(solution)/shard_map/reshape;reshape | solution.py:35
  107.2 7.9 %reduce_sum.57 = f32[9,32,32]{2,1,0:T(8,128)S(1)} reduce(f32[9,32,4,32,4]{4,3,2,1,0:T(8,128)} %reshape_reshape.14, f32[]{:T(128)} %constant.38.clone.1), dimensions={2,4}, to_apply=%region_4.5 | reduce | flops 138240 | bytes 626692 | tf_op jit(solution)/shard_map/reduce_sum | solution.py:35
  115.2 20.8 %reshape_reshape.15 = f32[9,32,4,32,4]{4,3,2,1,0:T(8,128)} reshape(f32[1,3,3,128,128]{4,3,2,1,0:T(8,128)S(1)} %copy.17) | data formatting | bytes 1179648 | tf_op jit(solution)/shard_map/reshape;reshape | solution.py:35
  136.0 8.0 %reduce_sum.58 = f32[9,32,32]{2,1,0:T(8,128)S(1)} reduce(f32[9,32,4,32,4]{4,3,2,1,0:T(8,128)} %reshape_reshape.15, f32[]{:T(128)} %constant.38.clone.1), dimensions={2,4}, to_apply=%region_5.6 | reduce | flops 138240 | bytes 626692 | tf_op jit(solution)/shard_map/reduce_sum | solution.py:35
  144.0 0.2 fusion.4
  144.2 0.2 fusion.5
  144.4 0.2 fusion.6
  144.6 0.2 fusion.7
  144.9 54.3 %psum.14 = f32[256]{0:T(256)S(1)} all-reduce(f32[256]{0:T(256)S(1)} %select_add_fusion), channel_id=1, replica_groups=mesh['snap'=16,'plane'=32] {'plane'}, use_global_device_ids=true, to_apply=%region_6.7 | all-reduce | flops 256 | bytes 2048 | tf_op jit(solution)/shard_map/psum | solution.py:61
  199.1 0.7 multiply_bitcast_fusion.4
  199.9 1.3 dynamic-slice
  201.8 109.0 %all-reduce.10.cloned.1.call-done = f32[2,1,32,256]{3,2,1,0:T(8,128)} async-done(((f32[2,1,32,256]{3,2,1,0:T(8,128)}), f32[2,1,32,256]{3,2,1,0:T(8,128)}) %all-reduce.10.cloned.1.call-update) | async-done | bytes 65552
  310.8 0.7 constant_dynamic-slice_fusion
  311.6 1.1 convolution_bitcast_fusion.4
  312.7 469.1 %all-reduce.8.cloned.1.call-done = f32[256,256]{1,0:T(8,128)} async-done(((f32[256,256]{1,0:T(8,128)}), f32[256,256]{1,0:T(8,128)}) %all-reduce.8.cloned.1.call-update) | async-done | bytes 262160 | tf_op jit(solution)/shard_map/psum | solution.py:73
  781.8 1.7 broadcast_multiply_fusion
  (30 shorter events, 0.4 us)
Async XLA Ops:
  7.2 136.9 %copy-start = (bf16[32,256]{1,0:T(8,128)(2,1)S(1)}, bf16[32,256]{1,0:T(8,128)(2,1)}, u32[]{:S(2)}) copy-start(bf16[32,256]{1,0:T(8,128)(2,1)} %param.14) | copy-start | bytes 49156
  7.2 6.3 copy-start.5
  7.2 12.0 %copy-start.3 = (f32[3,2,3,3]{3,1,2,0:T(2,128)S(1)}, f32[3,2,3,3]{3,1,2,0:T(2,128)}, u32[]{:S(2)}) copy-start(f32[3,2,3,3]{3,1,2,0:T(2,128)} %param.11) | copy-start | bytes 652
  7.2 12.3 %copy-start.7 = (bf16[1,2,4,128]{3,2,1,0:T(4,128)(2,1)S(1)}, bf16[1,2,4,128]{3,2,1,0:T(4,128)(2,1)}, u32[]{:S(2)}) copy-start(bf16[1,2,4,128]{3,2,1,0:T(4,128)(2,1)} %param.15) | copy-start | bytes 6148
  7.2 303.6 %all-reduce.10.cloned.1.call-start = ((), (), s32[]{:S(2)}) async-start(), calls=%async_computation.1 | async-start | bytes 131072
  9.1 16.5 %collective-permute-start = (bf16[1,3,128,128]{3,2,1,0:T(8,128)(2,1)S(1)}, bf16[1,3,128,128]{3,2,1,0:T(8,128)(2,1)S(1)}, u32[]{:S(2)}, u32[]{:S(2)}) collective-permute-start(bf16[1,3,128,128]{3,2,1,0:T(8,128)(2,1)S(1)} %get-tuple-element.29), channel_id=1, source_target_pairs={{1,0},{2,1},{3,2},{4,3},{5,4},{6,5},{7,6},{8,7},{9,8},{10,9},{11,1... | collective-permute-start | bytes 294920 | tf_op jit(solution)/shard_map/ppermute | solution.py:13
  10.4 15.2 %collective-permute-start.1 = (bf16[1,3,128,128]{3,2,1,0:T(8,128)(2,1)S(1)}, bf16[1,3,128,128]{3,2,1,0:T(8,128)(2,1)S(1)}, u32[]{:S(2)}, u32[]{:S(2)}) collective-permute-start(bf16[1,3,128,128]{3,2,1,0:T(8,128)(2,1)S(1)} %get-tuple-element.28), channel_id=1, source_target_pairs={{0,1},{1,2},{2,3},{3,4},{4,5},{5,6},{6,7},{7,8},{8,9},{9,10},{10,1... | collective-permute-start | bytes 294920 | tf_op jit(solution)/shard_map/ppermute | solution.py:13
  23.6 1.4 copy-start.6
  23.6 2.0 copy-start.1
  136.0 8.0 %copy-start.2 = (bf16[8,9,32,256]{3,2,1,0:T(8,128)(2,1)S(1)}, bf16[8,9,32,256]{3,2,1,0:T(8,128)(2,1)}, u32[]{:S(2)}) copy-start(bf16[8,9,32,256]{3,2,1,0:T(8,128)(2,1)} %param.13) | copy-start | bytes 3538948
  199.9 582.0 %all-reduce.8.cloned.1.call-start = ((), (), s32[]{:S(2)}) async-start(), calls=%async_computation | async-start | bytes 524288 | tf_op jit(solution)/shard_map/psum | solution.py:73
  311.6 471.9 %copy-start.4 = (f32[2,1,2,256]{3,2,1,0:T(2,128)}, f32[2,1,2,256]{3,2,1,0:T(2,128)S(1)}, u32[]{:S(2)}) copy-start(f32[2,1,2,256]{3,2,1,0:T(2,128)S(1)} %constant_dynamic-slice_fusion) | copy-start | bytes 12292
Sparse Core Ops, SparseCore 0:
  200.0 110.8 all-reduce.9
  316.9 464.9 all-reduce.7
where the time goes:
time: 791 us; the launch traced here: 790 us
  waiting for transfers between devices  578 us (73%)
  local copies, waits for them, and re-layouts  87.4 us (11%)
  blocking collectives  54.3 us (7%)
  other arithmetic  40.9 us (5%)
  between operations  23.3 us (3%)
    psum x1, waiting for transfers between devices, per_device(): gram = lax.psum(local_gram, ('snap', 'plane')) / jnp.float32(total_rows)  469 us
    unnamed x3, waiting for transfers between devices  109 us
    another operation x4, local copies, waits for them, and re-layouts, features(): filtered = grads.reshape(snaps, 9, zw // 4, 4, xw // 4, 4).mean(axis=(3, 5))  83.6 us
    psum x1, blocking collectives, per_device(): coef = lax.psum(coef, 'plane')  54.3 us
    reduce_sum x4, other arithmetic, features(): filtered = grads.reshape(snaps, 9, zw // 4, 4, xw // 4, 4).mean(axis=(3, 5))  31.8 us
  transfers between devices with their start and end apart: 4, of which 2 were waited for; matrix products, arithmetic and copies ran while one was open for 1% of the time, Pallas kernels for 0%

commit v1 on v0

--- a/solution.py
+++ b/solution.py
@@ -70,7 +70,7 @@
     total_rows = 2 * (X // 4) * (ZW // 4)
     flat = sketch.reshape(-1, sketch.shape[-1])
     local_gram = jnp.dot(flat.T, flat, precision=lax.Precision.HIGHEST)
-    gram = lax.psum(local_gram, ("snap", "plane")) / jnp.float32(total_rows)
+    gram = lax.psum(lax.psum(local_gram, "plane"), "snap") / jnp.float32(total_rows)
     return (sketch, gram)
 
 

time: 791 us -> 652 us (0.82)
  waiting for transfers between devices: 578 us -> 439 us
    psum x1 -> x2, waiting for transfers between devices: 469 us -> 330 us  [the longest x1 211 us: per_device(): lax.psum(local_gram, 'plane')]
    unnamed x3 -> x4, waiting for transfers between devices: 109 us -> 109 us
  transfers between devices with their start and end apart: 4 -> 5, of which waited for: 2 -> 3; matrix products, arithmetic and copies ran while one was open for 1% -> 1% of each run, Pallas kernels for 0% -> 0%
where the time goes in v1:
time: 652 us; the launch traced here: 651 us
  waiting for transfers between devices  439 us (67%)
  local copies, waits for them, and re-layouts  87.4 us (13%)
  blocking collectives  54.3 us (8%)
  other arithmetic  40.9 us (6%)
  between operations  23 us (4%)
    psum x1, waiting for transfers between devices, per_device(): lax.psum(local_gram, 'plane')  211 us
    psum x1, waiting for transfers between devices, per_device(): lax.psum(lax.psum(local_gram, 'plane'), 'snap') / jnp.float32(total_rows)  119 us
    unnamed x4, waiting for transfers between devices  109 us
    another operation x4, local copies, waits for them, and re-layouts, features(): filtered = grads.reshape(snaps, 9, zw // 4, 4, xw // 4, 4).mean(axis=(3, 5))  83.6 us
    psum x1, blocking collectives, per_device(): coef = lax.psum(coef, 'plane')  54.3 us
    reduce_sum x4, other arithmetic, features(): filtered = grads.reshape(snaps, 9, zw // 4, 4, xw // 4, 4).mean(axis=(3, 5))  31.8 us
  transfers between devices with their start and end apart: 5, of which 3 were waited for; matrix products, arithmetic and copies ran while one was open for 1% of the time, Pallas kernels for 0%

profile of v1, /device:TPU:2, one launch (start us, length us, event | category | flops | bytes accessed | tf_op | source)
XLA Modules:
  0.0 651.0 jit_solution(490046854737114340)
XLA Ops:
  7.9 1.2 fusion.21
  9.1 1.3 collective-permute-start
  10.4 3.0 collective-permute-start.1
  13.4 0.7 fusion.23
  19.2 0.2 slice_reduce_fusion.17
  19.5 0.1 reduce_sum.53
  22.2 1.3 add_bitcast_fusion.7
  23.6 1.3 add_bitcast_fusion.6
  24.9 0.7 fusion.22
  25.6 2.7 multiply_bitcast_fusion.3
  28.4 21.0 %reshape_reshape.12 = f32[9,32,4,32,4]{4,3,2,1,0:T(8,128)} reshape(f32[1,3,3,128,128]{4,3,2,1,0:T(8,128)S(1)} %copy.14) | data formatting | bytes 1179648 | tf_op jit(solution)/shard_map/reshape;reshape | solution.py:35
  49.5 7.9 %reduce_sum.55 = f32[9,32,32]{2,1,0:T(8,128)S(1)} reduce(f32[9,32,4,32,4]{4,3,2,1,0:T(8,128)} %reshape_reshape.12, f32[]{:T(128)} %constant.38.clone.1), dimensions={2,4}, to_apply=%region_2.3 | reduce | flops 138240 | bytes 626692 | tf_op jit(solution)/shard_map/reduce_sum | solution.py:35
  57.4 20.8 %reshape_reshape.13 = f32[9,32,4,32,4]{4,3,2,1,0:T(8,128)} reshape(f32[1,3,3,128,128]{4,3,2,1,0:T(8,128)S(1)} %copy.15) | data formatting | bytes 1179648 | tf_op jit(solution)/shard_map/reshape;reshape | solution.py:35
  78.3 7.9 %reduce_sum.56 = f32[9,32,32]{2,1,0:T(8,128)S(1)} reduce(f32[9,32,4,32,4]{4,3,2,1,0:T(8,128)} %reshape_reshape.13, f32[]{:T(128)} %constant.38.clone.1), dimensions={2,4}, to_apply=%region_3.4 | reduce | flops 138240 | bytes 626692 | tf_op jit(solution)/shard_map/reduce_sum | solution.py:35
  86.2 0.1 pad_maximum_fusion.2
  86.3 20.8 %reshape_reshape.14 = f32[9,32,4,32,4]{4,3,2,1,0:T(8,128)} reshape(f32[1,3,3,128,128]{4,3,2,1,0:T(8,128)S(1)} %copy.16) | data formatting | bytes 1179648 | tf_op jit(solution)/shard_map/reshape;reshape | solution.py:35
  107.2 7.9 %reduce_sum.57 = f32[9,32,32]{2,1,0:T(8,128)S(1)} reduce(f32[9,32,4,32,4]{4,3,2,1,0:T(8,128)} %reshape_reshape.14, f32[]{:T(128)} %constant.38.clone.1), dimensions={2,4}, to_apply=%region_4.5 | reduce | flops 138240 | bytes 626692 | tf_op jit(solution)/shard_map/reduce_sum | solution.py:35
  115.2 20.8 %reshape_reshape.15 = f32[9,32,4,32,4]{4,3,2,1,0:T(8,128)} reshape(f32[1,3,3,128,128]{4,3,2,1,0:T(8,128)S(1)} %copy.17) | data formatting | bytes 1179648 | tf_op jit(solution)/shard_map/reshape;reshape | solution.py:35
  136.0 8.0 %reduce_sum.58 = f32[9,32,32]{2,1,0:T(8,128)S(1)} reduce(f32[9,32,4,32,4]{4,3,2,1,0:T(8,128)} %reshape_reshape.15, f32[]{:T(128)} %constant.38.clone.1), dimensions={2,4}, to_apply=%region_5.6 | reduce | flops 138240 | bytes 626692 | tf_op jit(solution)/shard_map/reduce_sum | solution.py:35
  144.0 0.2 fusion.4
  144.2 0.2 fusion.5
  144.4 0.2 fusion.6
  144.6 0.2 fusion.7
  144.9 54.3 %psum.21 = f32[256]{0:T(256)S(1)} all-reduce(f32[256]{0:T(256)S(1)} %select_add_fusion), channel_id=1, replica_groups=mesh['snap'=16,'plane'=32] {'plane'}, use_global_device_ids=true, to_apply=%region_6.7 | all-reduce | flops 256 | bytes 2048 | tf_op jit(solution)/shard_map/psum | solution.py:61
  199.1 0.7 multiply_bitcast_fusion.4
  199.9 1.3 dynamic-slice
  201.8 109.0 %all-reduce.13.cloned.1.call-done = f32[2,1,32,256]{3,2,1,0:T(8,128)} async-done(((f32[2,1,32,256]{3,2,1,0:T(8,128)}), f32[2,1,32,256]{3,2,1,0:T(8,128)}) %all-reduce.13.cloned.1.call-update) | async-done | bytes 65552
  310.8 0.7 constant_dynamic-slice_fusion
  311.6 1.1 convolution_bitcast_fusion.4
  312.8 211.3 %all-reduce.9.cloned.1.call-done = f32[256,256]{1,0:T(8,128)} async-done(((f32[256,256]{1,0:T(8,128)}), f32[256,256]{1,0:T(8,128)}) %all-reduce.9.cloned.1.call-update) | async-done | bytes 262160 | tf_op jit(solution)/shard_map/psum | solution.py:73
  524.2 118.6 %all-reduce.11.cloned.1.call-done = f32[256,256]{1,0:T(8,128)} async-done(((f32[256,256]{1,0:T(8,128)}), f32[256,256]{1,0:T(8,128)}) %all-reduce.11.cloned.1.call-update) | async-done | bytes 262160 | tf_op jit(solution)/shard_map/psum | solution.py:73
  642.8 1.7 broadcast_multiply_fusion
  (33 shorter events, 0.6 us)
Async XLA Ops:
  7.2 136.9 %copy-start = (bf16[32,256]{1,0:T(8,128)(2,1)S(1)}, bf16[32,256]{1,0:T(8,128)(2,1)}, u32[]{:S(2)}) copy-start(bf16[32,256]{1,0:T(8,128)(2,1)} %param.14) | copy-start | bytes 49156
  7.2 6.3 copy-start.5
  7.2 12.0 %copy-start.3 = (f32[3,2,3,3]{3,1,2,0:T(2,128)S(1)}, f32[3,2,3,3]{3,1,2,0:T(2,128)}, u32[]{:S(2)}) copy-start(f32[3,2,3,3]{3,1,2,0:T(2,128)} %param.11) | copy-start | bytes 652
  7.2 12.3 %copy-start.7 = (bf16[1,2,4,128]{3,2,1,0:T(4,128)(2,1)S(1)}, bf16[1,2,4,128]{3,2,1,0:T(4,128)(2,1)}, u32[]{:S(2)}) copy-start(bf16[1,2,4,128]{3,2,1,0:T(4,128)(2,1)} %param.15) | copy-start | bytes 6148
  7.2 303.6 %all-reduce.13.cloned.1.call-start = ((), (), s32[]{:S(2)}) async-start(), calls=%async_computation.2 | async-start | bytes 131072
  9.1 16.5 %collective-permute-start = (bf16[1,3,128,128]{3,2,1,0:T(8,128)(2,1)S(1)}, bf16[1,3,128,128]{3,2,1,0:T(8,128)(2,1)S(1)}, u32[]{:S(2)}, u32[]{:S(2)}) collective-permute-start(bf16[1,3,128,128]{3,2,1,0:T(8,128)(2,1)S(1)} %get-tuple-element.29), channel_id=1, source_target_pairs={{1,0},{2,1},{3,2},{4,3},{5,4},{6,5},{7,6},{8,7},{9,8},{10,9},{11,1... | collective-permute-start | bytes 294920 | tf_op jit(solution)/shard_map/ppermute | solution.py:13
  10.4 15.2 %collective-permute-start.1 = (bf16[1,3,128,128]{3,2,1,0:T(8,128)(2,1)S(1)}, bf16[1,3,128,128]{3,2,1,0:T(8,128)(2,1)S(1)}, u32[]{:S(2)}, u32[]{:S(2)}) collective-permute-start(bf16[1,3,128,128]{3,2,1,0:T(8,128)(2,1)S(1)} %get-tuple-element.28), channel_id=1, source_target_pairs={{0,1},{1,2},{2,3},{3,4},{4,5},{5,6},{6,7},{7,8},{8,9},{9,10},{10,1... | collective-permute-start | bytes 294920 | tf_op jit(solution)/shard_map/ppermute | solution.py:13
  23.6 1.4 copy-start.6
  23.6 2.0 copy-start.1
  136.0 8.0 %copy-start.2 = (bf16[8,9,32,256]{3,2,1,0:T(8,128)(2,1)S(1)}, bf16[8,9,32,256]{3,2,1,0:T(8,128)(2,1)}, u32[]{:S(2)}) copy-start(bf16[8,9,32,256]{3,2,1,0:T(8,128)(2,1)} %param.13) | copy-start | bytes 3538948
  199.9 324.3 %all-reduce.9.cloned.1.call-start = ((), (), s32[]{:S(2)}) async-start(), calls=%async_computation | async-start | bytes 524288 | tf_op jit(solution)/shard_map/psum | solution.py:73
  311.6 332.9 %copy-start.4 = (f32[2,1,2,256]{3,2,1,0:T(2,128)}, f32[2,1,2,256]{3,2,1,0:T(2,128)S(1)}, u32[]{:S(2)}) copy-start(f32[2,1,2,256]{3,2,1,0:T(2,128)S(1)} %constant_dynamic-slice_fusion) | copy-start | bytes 12292
  312.7 330.1 %all-reduce.11.cloned.1.call-start = ((), (), s32[]{:S(2)}) async-start(), calls=%async_computation.1 | async-start | bytes 524288 | tf_op jit(solution)/shard_map/psum | solution.py:73
Sparse Core Ops, SparseCore 0:
  200.0 110.8 all-reduce.12
  313.7 210.3 all-reduce.8
  527.3 115.4 all-reduce.10
